TPU v7x, 256 devices: a whole 4x4x8 slice. The times are simulated.
256 devices in a mesh: elem: 16 (over z_lo, y, core), mode: 16 (over z_hi, x).
Axes of the slice: x: 4, y: 4, z: 8 (z_hi: 4, z_lo: 2; z = z_hi * 2 + z_lo), core: 2. Of those that a mesh axis runs over, the one named last changes fastest.
Arguments:
- coeff: float32 [64, 256, 2048], P(None, 'mode', 'elem'), as said below
- vel_axial: bfloat16 [64, 256, 2048], P('mode', None, 'elem'), may hold values from -3 to 3
- vel_radial: bfloat16 [64, 256, 2048], P('mode', None, 'elem'), may hold values from -3 to 3
- swirl_rate: bfloat16 [64, 256, 2048], P('mode', None, 'elem'), may hold values from -3 to 3
- col_width: float32 [128], P('elem'), may hold values from 0.5 to 2
- row_height: float32 [16], replicated, may hold values from 0.5 to 2
- stiffness: float32 [64, 64], replicated
- stiff_elem: float32 [2048], P('elem'), may hold values from 0.5 to 4
- mass: float32 [64, 2048], P(None, 'elem'), may hold values from 0.25 to 1
- azim_weight: float32 [64, 2048], P(None, 'elem'), may hold values from 0.5 to 8
- wall_flag: int32 [128], P('elem'), may hold values 0 or 1
- transfer: float32 [128], P('elem'), may hold values from 0.5 to 4
Outputs:
- solution: float32 [64, 256, 2048], P(None, 'mode', 'elem')
Inputs may be any that keep to these rules, and one draw needn't show every extreme that they name: `coeff`: every grid point that neighbouring elements share has the same coefficients in each of them.
All inputs are finite; a program needn't handle non-finite values. No bound on the sum of `wall_flag` on one device may be relied on, other than what follows from the above.
Results may differ from a plain program's by a relative error of at most 0.0003.
Values sent between devices are 32-bit elements; how exact they have to be, the bound alone decides.
A program may use at most 64 MiB of HBM per device.

v0:
```python
import functools

import jax
import jax.numpy as jnp
import ml_dtypes
import numpy as np
from jax import lax
from jax.experimental import pallas as pl
from jax.experimental.pallas import tpu as pltpu
from jax.sharding import PartitionSpec as P

MESH = pl.DeviceIdType.MESH
SIDE = 8
NODES = 64
SWEEPS = 3
INV_STEP = 2.0
RELAX = 0.8
RING = 4
F32 = jnp.float32
BF16 = jnp.bfloat16


def cheb_matrix(side_count):
    points = np.cos(np.pi * np.arange(side_count) / (side_count - 1))
    weights = np.ones(side_count)
    weights[0] = weights[-1] = 2.0
    weights = weights * (-1.0) ** np.arange(side_count)
    table = np.zeros((side_count, side_count))
    for row in range(side_count):
        for col in range(side_count):
            if row != col:
                table[row, col] = weights[row] / weights[col] / (points[row] - points[col])
        table[row, row] = -np.sum(table[row])
    return table


def split_table(table):
    high = table.astype(np.float32).astype(ml_dtypes.bfloat16)
    low = (table - high.astype(np.float64)).astype(np.float32).astype(ml_dtypes.bfloat16)
    return [high, low]


def fourier_tables(planes):
    q = np.arange(planes)
    k = (q + 1) // 2
    angle = 2.0 * np.pi / planes * ((k[:, None] * np.arange(planes)[None, :]) % planes)
    sine = ((q % 2 == 0) & (q > 0))[:, None]
    wave = k[:, None].astype(np.float64)
    basis = np.where(sine, np.sin(angle), np.cos(angle))
    slope = np.where(sine, wave * np.cos(angle), -wave * np.sin(angle))
    norm = np.where((q == 0) | (q == planes - 1), 1.0, 2.0) / planes
    forward = basis * norm[:, None]
    return np.stack(split_table(slope.T) + split_table(basis.T) + split_table(forward))


def split(value):
    high = value.astype(BF16)
    return high, (value - high.astype(F32)).astype(BF16)


def dot3(tab_high, tab_low, value):
    high, low = split(value)
    total = jnp.dot(tab_high, high, preferred_element_type=F32)
    total += jnp.dot(tab_high, low, preferred_element_type=F32)
    return total + jnp.dot(tab_low, high, preferred_element_type=F32)


def kernel(
    modes, coeff, vel_t, vel_y, vel_x, tables, col_width, row_height, stiff, stiff_elem, mass, azim,
    wall_flag, transfer, out,
    vel, tab, grad_y, zbuf, xbuf, hat, adv, fld, lam, rate, load, res, hsend, hrecv,
    local_sem, zs, zr, xs, xr, bs, br, hs, hr,
):
    s, m = lax.axis_index("elem"), lax.axis_index("mode")
    elems = lax.axis_size("elem")
    z, x = m // RING, m % RING
    cheb = cheb_matrix(SIDE)

    fetches = [
        pltpu.make_async_copy(src, dst, local_sem.at[i])
        for i, (src, dst) in enumerate(
            [(vel_t, vel.at[0]), (vel_y, vel.at[1]), (vel_x, vel.at[2]), (tables, tab)]
        )
    ]
    for fetch in fetches:
        fetch.start()

    left, right = lax.rem(s + elems - 1, elems), lax.rem(s + 1, elems)
    barrier = pltpu.get_barrier_semaphore()
    for step in range(1, RING):
        pl.semaphore_signal(
            barrier, inc=1, device_id={"mode": (z + step) % RING * RING + x}, device_id_type=MESH
        )
        pl.semaphore_signal(
            barrier, inc=1, device_id={"mode": z * RING + (x + step) % RING}, device_id_type=MESH
        )
    for other in (left, right):
        pl.semaphore_signal(barrier, inc=1, device_id={"elem": other}, device_id_type=MESH)

    lane = lax.broadcasted_iota(jnp.int32, (1, 128), 1)
    col, row = lane // 16, lane % 16
    width = jnp.zeros((1, 128), F32)
    flow = jnp.zeros((1, 128), F32)
    for a in range(8):
        width = jnp.where(col == a, col_width[a], width)
        flow = jnp.where(col == a, wall_flag[a].astype(F32) * transfer[a], flow)
    flow = jnp.where(row == 0, flow, 0.0)
    height = jnp.zeros((1, 128), F32)
    for b in range(16):
        height = jnp.where(row == b, row_height[b], height)
    scale_x = 2.0 / width
    scale_y = 2.0 / height

    @pl.loop(0, SIDE)
    def _(i):
        start = pl.multiple_of(i * 16, 16)
        cells = [coeff[pl.ds(start + j * 128, 16), :] for j in range(SIDE)]
        for j in range(SIDE):
            total = cheb[j, 0] * cells[0]
            for k in range(1, SIDE):
                total += cheb[j, k] * cells[k]
            grad_y[pl.ds(start + j * 128, 16), :] = total * scale_y

    pl.semaphore_wait(barrier, 2 * (RING - 1) + 2)

    own_row = x // 2
    rows = (1 - own_row, own_row)
    zcopy = {}

    def start_z(d, rr):
        target = (z + d) % RING
        block = pl.ds(pl.multiple_of((target * 2 + rows[rr]) * 128, 128), 128)
        for kind, src in ((0, coeff), (1, grad_y)):
            copy = pltpu.make_async_remote_copy(
                src_ref=src.at[block],
                dst_ref=zbuf.at[z, rows[rr], kind],
                send_sem=zs.at[d - 1, rr, kind],
                recv_sem=zr.at[d - 1, rr, kind],
                device_id={"mode": target * RING + x},
                device_id_type=MESH,
            )
            copy.start()
            zcopy[d, rr, kind] = copy

    for rr in range(2):
        start_z(1, rr)
        start_z(3, rr)
    for rr in range(2):
        start_z(2, rr)

    partner = {1: x + 1 - 2 * (x % 2), 2: (x + 2) % RING, 3: RING - 1 - x}
    xcopy = {}

    def pass_on(k, source, rr):
        line = rows[rr]
        cells = [zbuf[source, line, 0, 16 * i : 16 * i + 16, :] for i in range(SIDE)]
        for i in range(SIDE):
            total = cheb[i, 0] * cells[0]
            for j in range(1, SIDE):
                total += cheb[i, j] * cells[j]
            zbuf[source, line, 2, 16 * i : 16 * i + 16, :] = total * scale_x
        for mask in (2, 3) if rr == 0 else (1,):
            target = partner[mask]
            copy = pltpu.make_async_remote_copy(
                src_ref=zbuf.at[source, line, :, pl.ds(pl.multiple_of(target % 2 * 64, 64), 64)],
                dst_ref=xbuf.at[source * RING + x],
                send_sem=xs.at[k, mask - 1],
                recv_sem=xr.at[k, mask - 1],
                device_id={"mode": z * RING + target},
                device_id_type=MESH,
            )
            copy.start()
            xcopy[k, mask] = copy
        if rr == 1:
            xbuf[source * RING + x] = zbuf[
                source, line, :, pl.ds(pl.multiple_of(x % 2 * 64, 64), 64), :
            ]

    for rr in range(2):
        block = pl.ds(pl.multiple_of((z * 2 + rows[rr]) * 128, 128), 128)
        zbuf[z, rows[rr], 0] = coeff[block, :]
        zbuf[z, rows[rr], 1] = grad_y[block, :]
        pass_on(0, z, rr)

    elem_scale = stiff_elem[...]
    ones = mass[...]
    weights = azim[...]
    node = lax.broadcasted_iota(jnp.int32, (NODES, 128), 0)
    wall = jnp.where(node < SIDE, jnp.broadcast_to(flow, (NODES, 128)), 0.0)
    stiffness = stiff[...]
    on_diag = lax.broadcasted_iota(jnp.int32, (NODES, NODES), 0) == lax.broadcasted_iota(
        jnp.int32, (NODES, NODES), 1
    )
    stiff_diag = jnp.sum(jnp.where(on_diag, stiffness, 0.0), axis=1, keepdims=True) * elem_scale
    stiff_high, stiff_low = split(stiffness)

    def helmholtz(pair):
        both = jnp.concatenate([fld[2 * pair], fld[2 * pair + 1]], axis=1)
        spread = dot3(stiff_high, stiff_low, both)
        return [
            elem_scale * spread[:, 128 * h : 128 * h + 128] + lam[2 * pair + h] * fld[2 * pair + h]
            for h in range(2)
        ]

    for q in range(modes):
        wave = ((m * modes + q + 1) // 2).astype(F32) * (2.0 / (modes * RING * RING))
        lam[q] = (INV_STEP + (wave * wave) * weights) * ones + wall
        rate[q] = stiff_diag + lam[q]
        fld[q] = coeff[pl.ds(q, NODES, stride=modes), :]

    def send_edges(values, turn):
        for g in range(2):
            first = jnp.zeros((SIDE, 128), F32)
            last = jnp.zeros((SIDE, 128), F32)
            for k in range(8):
                q = 8 * g + k
                low = values[q, pl.ds(0, SIDE, stride=SIDE), :]
                high = values[q, pl.ds(SIDE - 1, SIDE, stride=SIDE), :]
                if k > 0:
                    low = pltpu.roll(low, 16 * k, 1)
                if k < 7:
                    high = pltpu.roll(high, 16 * k + 16, 1)
                first = jnp.where(col == k, low, first)
                last = jnp.where(col == k, high, last)
            hsend[turn, 0, g] = first
            hsend[turn, 1, g] = last
        copies = []
        for side, other in ((0, left), (1, right)):
            copy = pltpu.make_async_remote_copy(
                src_ref=hsend.at[turn, side],
                dst_ref=hrecv.at[turn, 1 - side],
                send_sem=hs.at[turn, side],
                recv_sem=hr.at[turn, 1 - side],
                device_id={"elem": other},
                device_id_type=MESH,
            )
            copy.start()
            copies.append(copy)
        return copies

    has_left = (s > 0).astype(F32)
    has_right = (s < elems - 1).astype(F32)

    def assemble(values, turn, copies):
        for copy in copies:
            copy.wait()
        for g in range(2):
            from_left = hrecv[turn, 0, g] * has_left
            from_right = hrecv[turn, 1, g] * has_right
            for k in range(8):
                q = 8 * g + k
                low = values[q, pl.ds(0, SIDE, stride=SIDE), :]
                high = values[q, pl.ds(SIDE - 1, SIDE, stride=SIDE), :]
                near = pltpu.roll(from_left, 128 - 16 * k, 1) if k > 0 else from_left
                far = pltpu.roll(from_right, 112 - 16 * k, 1) if k < 7 else from_right
                values[q, pl.ds(0, SIDE, stride=SIDE), :] = low + jnp.where(
                    col == 0, near, pltpu.roll(high, 16, 1)
                )
                values[q, pl.ds(SIDE - 1, SIDE, stride=SIDE), :] = high + jnp.where(
                    col == 7, far, pltpu.roll(low, 112, 1)
                )
                lower = values[q, 0:SIDE, :]
                upper = values[q, NODES - SIDE : NODES, :]
                values[q, 0:SIDE, :] = lower + jnp.where(row > 0, pltpu.roll(upper, 1, 1), 0.0)
                values[q, NODES - SIDE : NODES, :] = upper + jnp.where(
                    row < 15, pltpu.roll(lower, 127, 1), 0.0
                )

    diag_copies = send_edges(rate, 0)
    for pair in range(modes // 2):
        for h, applied in enumerate(helmholtz(pair)):
            q = 2 * pair + h
            load[q] = INV_STEP * ones * fld[q]
            res[q] = load[q] - applied
    assemble(rate, 0, diag_copies)
    for q in range(modes):
        rate[q] = RELAX / rate[q]

    for k, d in ((1, 1), (2, 3), (3, 2)):
        for rr in range(2):
            for kind in range(2):
                zcopy[d, rr, kind].wait_recv()
            pass_on(k, (z - d + RING) % RING, rr)

    for fetch in fetches:
        fetch.wait()
    for copy in xcopy.values():
        copy.wait_recv()

    for pair in range(2):
        advect = None
        for kind in range(3):
            pieces = [
                xbuf[:, kind, 32 * pair + 16 * h : 32 * pair + 16 * h + 16, :].reshape(-1, 128)
                for h in range(2)
            ]
            which = 0 if kind == 0 else 2
            phys = dot3(tab[which], tab[which + 1], jnp.concatenate(pieces, axis=1))
            speed = jnp.concatenate([vel[kind, 2 * pair], vel[kind, 2 * pair + 1]], axis=1)
            term = speed.astype(F32) * phys
            advect = term if advect is None else advect + term
        back = dot3(tab[4], tab[5], advect)
        for h in range(2):
            for t in range(RING * RING):
                at = t * 64 + (2 * pair + h) * 16
                hat[at : at + 16, :] = back[16 * t : 16 * t + 16, 128 * h : 128 * h + 128]

    mine = pl.ds(pl.multiple_of(m * 64, 64), 64)
    bcopy = []
    for d in range(1, RING * RING):
        target = (m + d) % (RING * RING)
        copy = pltpu.make_async_remote_copy(
            src_ref=hat.at[pl.ds(pl.multiple_of(target * 64, 64), 64)],
            dst_ref=adv.at[mine],
            send_sem=bs.at[d - 1],
            recv_sem=br.at[d - 1],
            device_id={"mode": target},
            device_id_type=MESH,
        )
        copy.start()
        bcopy.append(copy)
    adv[mine, :] = hat[mine, :]
    for copy in bcopy:
        copy.wait_recv()

    for q in range(modes):
        push = ones * adv[pl.ds(q, NODES, stride=modes), :]
        load[q] = load[q] - push
        res[q] = res[q] - push

    for sweep in range(SWEEPS):
        assemble(res, sweep + 1, send_edges(res, sweep + 1))
        if sweep < SWEEPS - 1:
            for q in range(modes):
                fld[q] = fld[q] + rate[q] * res[q]
            for pair in range(modes // 2):
                for h, applied in enumerate(helmholtz(pair)):
                    res[2 * pair + h] = load[2 * pair + h] - applied
        else:
            for q in range(modes):
                out[pl.ds(q, NODES, stride=modes), :] = fld[q] + rate[q] * res[q]

    for copies in (zcopy, xcopy):
        for copy in copies.values():
            copy.wait_send()
    for copy in bcopy:
        copy.wait_send()


def local(
    tables, coeff, vel_axial, vel_radial, swirl_rate, col_width, row_height, stiffness, stiff_elem,
    mass, azim_weight, wall_flag, transfer,
):
    modes = coeff.shape[1]
    planes = vel_axial.shape[1]
    vmem = pl.BlockSpec(memory_space=pltpu.VMEM)
    smem = pl.BlockSpec(memory_space=pltpu.SMEM)
    anywhere = pl.BlockSpec(memory_space=pl.ANY)
    dma = pltpu.SemaphoreType.DMA
    field = pltpu.VMEM((modes, NODES, 128), F32)
    flat = pltpu.VMEM((NODES * modes, 128), F32)
    result = pl.pallas_call(
        functools.partial(kernel, modes),
        out_shape=jax.ShapeDtypeStruct((NODES * modes, 128), F32),
        in_specs=[
            vmem, anywhere, anywhere, anywhere, anywhere, smem, smem, vmem, vmem, vmem, vmem, smem,
            smem,
        ],
        out_specs=vmem,
        scratch_shapes=[
            pltpu.VMEM((3, 4, planes, 128), BF16),
            pltpu.VMEM(tables.shape, BF16),
            flat,
            pltpu.VMEM((RING, 2, 3, 8 * modes, 128), F32),
            pltpu.VMEM((RING * RING, 3, 4 * modes, 128), F32),
            flat,
            flat,
            field,
            field,
            field,
            field,
            field,
            pltpu.VMEM((SWEEPS + 1, 2, 2, SIDE, 128), F32),
            pltpu.VMEM((SWEEPS + 1, 2, 2, SIDE, 128), F32),
            dma((4,)),
            dma((3, 2, 2)),
            dma((3, 2, 2)),
            dma((4, 3)),
            dma((4, 3)),
            dma((15,)),
            dma((15,)),
            dma((SWEEPS + 1, 2)),
            dma((SWEEPS + 1, 2)),
        ],
        compiler_params=pltpu.CompilerParams(collective_id=0, has_side_effects=True),
    )(
        coeff.reshape(NODES * modes, 128),
        swirl_rate,
        vel_radial,
        vel_axial,
        jnp.asarray(tables),
        col_width,
        row_height,
        stiffness,
        stiff_elem.reshape(1, 128),
        mass,
        azim_weight,
        wall_flag,
        transfer,
    )
    return result.reshape(coeff.shape)


def solution(mesh):
    tables = fourier_tables(256)
    return jax.shard_map(
        functools.partial(local, tables),
        mesh=mesh,
        in_specs=(
            P(None, "mode", "elem"),
            P("mode", None, "elem"),
            P("mode", None, "elem"),
            P("mode", None, "elem"),
            P("elem"),
            P(),
            P(),
            P("elem"),
            P(None, "elem"),
            P(None, "elem"),
            P("elem"),
            P("elem"),
        ),
        out_specs=P(None, "mode", "elem"),
        check_vma=False,
    )
```

profile of v0, /device:TPU:1, one launch (start us, length us, event | category | flops | bytes accessed | tf_op | source)
XLA Modules:
  0.0 72.7 jit_solution(7091164402833942316)
XLA Ops:
  0.0 70.8 %shard_map.127 = f32[1024,128]{1,0:T(8,128)} custom-call(f32[1024,128]{1,0:T(8,128)} %bitcast.4, bf16[4,256,128]{2,1,0:T(8,128)(2,1)} %vel_t.1, bf16[4,256,128]{2,1,0:T(8,128)(2,1)} %vel_y.1, bf16[4,256,128]{2,1,0:T(8,128)(2,1)} %vel_x.1, bf16[6,256,256]{2,1,0:T(8,128)(2,1)} %constant.2.clone.tables, f32[8]{0:T(128)} %col_width.1, f32[16]{0:T(128)} %row_height.1, ...), custom_call_target="tpu_custom_call" | custom-call | tf_op jit(solution)/shard_map/pallas_call | solution.py:362
  70.8 1.9 %copy.15 = f32[64,16,128]{2,1,0:T(8,128)} copy(f32[64,16,128]{2,1,0:T(8,128)} %bitcast.3) | data formatting | bytes 1048576
where the time goes:
time: 72.8 us; the launch traced here: 72.7 us
  Pallas kernels  70.8 us (97%)
  local copies, waits for them, and re-layouts  1.87 us (3%)
    pallas_call x1, Pallas kernels, local(): pl.pallas_call(functools.partial(kernel, modes), out_shape=jax.ShapeDtype...  70.8 us
    unnamed x1, local copies, waits for them, and re-layouts  1.87 us

commit v1 on v0

--- a/solution.py
+++ b/solution.py
@@ -66,24 +66,16 @@
 
 
 def kernel(
-    modes, coeff, vel_t, vel_y, vel_x, tables, col_width, row_height, stiff, stiff_elem, mass, azim,
-    wall_flag, transfer, out,
-    vel, tab, grad_y, zbuf, xbuf, hat, adv, fld, lam, rate, load, res, hsend, hrecv,
-    local_sem, zs, zr, xs, xr, bs, br, hs, hr,
+    modes, coeff_in, vel_t, vel_y, vel_x, tables, width_in, height_in, stiff_in, elem_in, mass_in,
+    azim_in, flag_in, transfer_in, out,
+    coeff, col_width, row_height, stiff, stiff_elem, mass, azim, wall_flag, transfer,
+    vel, tab, grad_y, zbuf, xbuf, hat, adv, fld, lam, rate, res, inc, work,
+    hsend, hrecv, psend, precv, tsend, halo, far, beside, local_sem, zs, zr, xs, xr, bs, br, hs, hr,
 ):
     s, m = lax.axis_index("elem"), lax.axis_index("mode")
     elems = lax.axis_size("elem")
     z, x = m // RING, m % RING
     cheb = cheb_matrix(SIDE)
-
-    fetches = [
-        pltpu.make_async_copy(src, dst, local_sem.at[i])
-        for i, (src, dst) in enumerate(
-            [(vel_t, vel.at[0]), (vel_y, vel.at[1]), (vel_x, vel.at[2]), (tables, tab)]
-        )
-    ]
-    for fetch in fetches:
-        fetch.start()
 
     left, right = lax.rem(s + elems - 1, elems), lax.rem(s + 1, elems)
     barrier = pltpu.get_barrier_semaphore()
@@ -97,14 +89,42 @@
     for other in (left, right):
         pl.semaphore_signal(barrier, inc=1, device_id={"elem": other}, device_id_type=MESH)
 
+    def fetch(pairs):
+        copies = [
+            pltpu.make_async_copy(src, dst, local_sem.at[i]) for i, (src, dst) in pairs
+        ]
+        for copy in copies:
+            copy.start()
+        return copies
+
+    early = fetch(
+        enumerate([(coeff_in, coeff), (height_in, row_height), (width_in, col_width)])
+    )
+    later = fetch(
+        enumerate(
+            [
+                (stiff_in, stiff),
+                (elem_in, stiff_elem),
+                (mass_in, mass),
+                (azim_in, azim),
+                (flag_in, wall_flag),
+                (transfer_in, transfer),
+                (vel_t, vel.at[0]),
+                (vel_y, vel.at[1]),
+                (vel_x, vel.at[2]),
+                (tables, tab),
+            ],
+            3,
+        )
+    )
+    for copy in early:
+        copy.wait()
+
     lane = lax.broadcasted_iota(jnp.int32, (1, 128), 1)
     col, row = lane // 16, lane % 16
     width = jnp.zeros((1, 128), F32)
-    flow = jnp.zeros((1, 128), F32)
     for a in range(8):
         width = jnp.where(col == a, col_width[a], width)
-        flow = jnp.where(col == a, wall_flag[a].astype(F32) * transfer[a], flow)
-    flow = jnp.where(row == 0, flow, 0.0)
     height = jnp.zeros((1, 128), F32)
     for b in range(16):
         height = jnp.where(row == b, row_height[b], height)
@@ -182,6 +202,12 @@
         zbuf[z, rows[rr], 1] = grad_y[block, :]
         pass_on(0, z, rr)
 
+    for copy in later[:6]:
+        copy.wait()
+    flow = jnp.zeros((1, 128), F32)
+    for a in range(8):
+        flow = jnp.where(col == a, wall_flag[a].astype(F32) * transfer[a], flow)
+    flow = jnp.where(row == 0, flow, 0.0)
     elem_scale = stiff_elem[...]
     ones = mass[...]
     weights = azim[...]
@@ -194,13 +220,9 @@
     stiff_diag = jnp.sum(jnp.where(on_diag, stiffness, 0.0), axis=1, keepdims=True) * elem_scale
     stiff_high, stiff_low = split(stiffness)
 
-    def helmholtz(pair):
-        both = jnp.concatenate([fld[2 * pair], fld[2 * pair + 1]], axis=1)
-        spread = dot3(stiff_high, stiff_low, both)
-        return [
-            elem_scale * spread[:, 128 * h : 128 * h + 128] + lam[2 * pair + h] * fld[2 * pair + h]
-            for h in range(2)
-        ]
+    def spread(first, second):
+        both = dot3(stiff_high, stiff_low, jnp.concatenate([first, second], axis=1))
+        return both[:, :128], both[:, 128:]
 
     for q in range(modes):
         wave = ((m * modes + q + 1) // 2).astype(F32) * (2.0 / (modes * RING * RING))
@@ -208,29 +230,22 @@
         rate[q] = stiff_diag + lam[q]
         fld[q] = coeff[pl.ds(q, NODES, stride=modes), :]
 
-    def send_edges(values, turn):
-        for g in range(2):
-            first = jnp.zeros((SIDE, 128), F32)
-            last = jnp.zeros((SIDE, 128), F32)
-            for k in range(8):
-                q = 8 * g + k
-                low = values[q, pl.ds(0, SIDE, stride=SIDE), :]
-                high = values[q, pl.ds(SIDE - 1, SIDE, stride=SIDE), :]
-                if k > 0:
-                    low = pltpu.roll(low, 16 * k, 1)
-                if k < 7:
-                    high = pltpu.roll(high, 16 * k + 16, 1)
-                first = jnp.where(col == k, low, first)
-                last = jnp.where(col == k, high, last)
-            hsend[turn, 0, g] = first
-            hsend[turn, 1, g] = last
+    first_nodes = pl.ds(0, SIDE, stride=SIDE)
+    last_nodes = pl.ds(SIDE - 1, SIDE, stride=SIDE)
+    has_left = (s > 0).astype(F32)
+    has_right = (s < elems - 1).astype(F32)
+
+    def turn(value, shift):
+        return pltpu.roll(value, shift % 128, 1) if shift % 128 else value
+
+    def swap(mine, theirs, turn_id):
         copies = []
         for side, other in ((0, left), (1, right)):
             copy = pltpu.make_async_remote_copy(
-                src_ref=hsend.at[turn, side],
-                dst_ref=hrecv.at[turn, 1 - side],
-                send_sem=hs.at[turn, side],
-                recv_sem=hr.at[turn, 1 - side],
+                src_ref=mine.at[side],
+                dst_ref=theirs.at[1 - side],
+                send_sem=hs.at[turn_id, side],
+                recv_sem=hr.at[turn_id, 1 - side],
                 device_id={"elem": other},
                 device_id_type=MESH,
             )
@@ -238,43 +253,101 @@
             copies.append(copy)
         return copies
 
-    has_left = (s > 0).astype(F32)
-    has_right = (s < elems - 1).astype(F32)
-
-    def assemble(values, turn, copies):
-        for copy in copies:
-            copy.wait()
-        for g in range(2):
-            from_left = hrecv[turn, 0, g] * has_left
-            from_right = hrecv[turn, 1, g] * has_right
-            for k in range(8):
-                q = 8 * g + k
-                low = values[q, pl.ds(0, SIDE, stride=SIDE), :]
-                high = values[q, pl.ds(SIDE - 1, SIDE, stride=SIDE), :]
-                near = pltpu.roll(from_left, 128 - 16 * k, 1) if k > 0 else from_left
-                far = pltpu.roll(from_right, 112 - 16 * k, 1) if k < 7 else from_right
-                values[q, pl.ds(0, SIDE, stride=SIDE), :] = low + jnp.where(
-                    col == 0, near, pltpu.roll(high, 16, 1)
-                )
-                values[q, pl.ds(SIDE - 1, SIDE, stride=SIDE), :] = high + jnp.where(
-                    col == 7, far, pltpu.roll(low, 112, 1)
-                )
-                lower = values[q, 0:SIDE, :]
-                upper = values[q, NODES - SIDE : NODES, :]
-                values[q, 0:SIDE, :] = lower + jnp.where(row > 0, pltpu.roll(upper, 1, 1), 0.0)
-                values[q, NODES - SIDE : NODES, :] = upper + jnp.where(
-                    row < 15, pltpu.roll(lower, 127, 1), 0.0
-                )
-
-    diag_copies = send_edges(rate, 0)
+    def join_rows(values, q):
+        lower = values[q, 0:SIDE, :]
+        upper = values[q, NODES - SIDE : NODES, :]
+        values[q, 0:SIDE, :] = lower + jnp.where(row > 0, turn(upper, 1), 0.0)
+        values[q, NODES - SIDE : NODES, :] = upper + jnp.where(row < 15, turn(lower, -1), 0.0)
+
+    for g in range(2):
+        first = jnp.zeros((SIDE, 128), F32)
+        last = jnp.zeros((SIDE, 128), F32)
+        for k in range(8):
+            first = jnp.where(col == k, turn(rate[8 * g + k, first_nodes, :], 16 * k), first)
+            last = jnp.where(col == k, turn(rate[8 * g + k, last_nodes, :], 16 * k + 16), last)
+        hsend[0, g] = first
+        hsend[1, g] = last
+    diag_copies = swap(hsend, hrecv, 0)
     for pair in range(modes // 2):
-        for h, applied in enumerate(helmholtz(pair)):
+        applied = spread(fld[2 * pair], fld[2 * pair + 1])
+        for h in range(2):
             q = 2 * pair + h
-            load[q] = INV_STEP * ones * fld[q]
-            res[q] = load[q] - applied
-    assemble(rate, 0, diag_copies)
+            res[q] = (INV_STEP * ones - lam[q]) * fld[q] - elem_scale * applied[h]
+    for copy in diag_copies:
+        copy.wait()
     for q in range(modes):
+        g, k = q // 8, q % 8
+        low, high = rate[q, first_nodes, :], rate[q, last_nodes, :]
+        near = turn(hrecv[0, g] * has_left, -16 * k)
+        past = turn(hrecv[1, g] * has_right, 112 - 16 * k)
+        rate[q, first_nodes, :] = low + jnp.where(col == 0, near, turn(high, 16))
+        rate[q, last_nodes, :] = high + jnp.where(col == 7, past, turn(low, -16))
+        join_rows(rate, q)
         rate[q] = RELAX / rate[q]
+
+    quad = lane // 32
+    outer = col % 2
+
+    def pack(values, send, slot):
+        for g in range(modes // 4):
+            for side in range(2):
+                total = None
+                for k in range(4):
+                    piece = turn(values[4 * g + k], 32 * k + 32 * side)
+                    total = piece if total is None else jnp.where(quad == k, piece, total)
+                send[side, slot + g] = total
+
+    pack(lam, psend, 0)
+    pack(rate, psend, 4)
+    for side in range(2):
+        total = None
+        for k in range(4):
+            piece = turn(elem_scale, 32 * k + 32 * side)
+            total = piece if total is None else jnp.where(quad == k, piece, total)
+        psend[side, 8] = jnp.broadcast_to(total, (NODES, 128))
+    halo_copies = swap(psend, precv, 1)
+
+    def join_inner(values):
+        for q in range(modes):
+            low, high = values[q, first_nodes, :], values[q, last_nodes, :]
+            values[q, first_nodes, :] = low + jnp.where(col == 0, 0.0, turn(high, 16))
+            values[q, last_nodes, :] = high + jnp.where(col == 7, 0.0, turn(low, -16))
+
+    def join_halo(values, beside, inner, both):
+        for g in range(modes // 4):
+            left_low, left_high = beside[0, g, first_nodes, :], beside[0, g, last_nodes, :]
+            right_low, right_high = beside[1, g, first_nodes, :], beside[1, g, last_nodes, :]
+            add_left = turn(left_low, -16)
+            add_right = turn(right_high, 16)
+            for k in range(4):
+                q = 4 * g + k
+                low, high = values[q, first_nodes, :], values[q, last_nodes, :]
+                near = turn(left_high * has_left, -32 * k - 16)
+                past = turn(right_low * has_right, 112 - 32 * k)
+                values[q, first_nodes, :] = jnp.where(col == 0, low + near, low)
+                values[q, last_nodes, :] = jnp.where(col == 7, high + past, high)
+                if both:
+                    add_left = jnp.where(col == 2 * k + 1, turn(low, 32 * k + 16), add_left)
+                    add_right = jnp.where(col == 2 * k, turn(high, 32 * k + 16), add_right)
+            if both:
+                if not inner:
+                    add_left = jnp.where(outer == 1, add_left, 0.0)
+                    add_right = jnp.where(outer == 0, add_right, 0.0)
+                beside[0, g, last_nodes, :] = left_high + add_left
+                beside[1, g, first_nodes, :] = right_low + add_right
+                if inner:
+                    beside[0, g, first_nodes, :] = left_low + jnp.where(
+                        outer == 1, turn(left_high, 16), 0.0
+                    )
+                    beside[1, g, last_nodes, :] = right_high + jnp.where(
+                        outer == 0, turn(right_low, -16), 0.0
+                    )
+        for q in range(modes):
+            join_rows(values, q)
+        if both:
+            for side in range(2):
+                for g in range(modes // 4):
+                    join_rows(beside.at[side], g)
 
     for k, d in ((1, 1), (2, 3), (3, 2)):
         for rr in range(2):
@@ -282,8 +355,8 @@
                 zcopy[d, rr, kind].wait_recv()
             pass_on(k, (z - d + RING) % RING, rr)
 
-    for fetch in fetches:
-        fetch.wait()
+    for copy in later[6:]:
+        copy.wait()
     for copy in xcopy.values():
         copy.wait_recv()
 
@@ -324,21 +397,46 @@
         copy.wait_recv()
 
     for q in range(modes):
-        push = ones * adv[pl.ds(q, NODES, stride=modes), :]
-        load[q] = load[q] - push
-        res[q] = res[q] - push
-
-    for sweep in range(SWEEPS):
-        assemble(res, sweep + 1, send_edges(res, sweep + 1))
+        res[q] = res[q] - ones * adv[pl.ds(q, NODES, stride=modes), :]
+    join_inner(res)
+    pack(res, tsend, 0)
+    for copy in halo_copies:
+        copy.wait()
+    for copy in swap(tsend, halo, 2):
+        copy.wait()
+    join_halo(res, halo, False, True)
+
+    for q in range(modes):
+        inc[q] = rate[q] * res[q]
+    for side in range(2):
+        for g in range(modes // 4):
+            far[side, g] = precv[side, 4 + g] * halo[side, g]
+    for sweep in range(1, SWEEPS):
+        for pair in range(modes // 2):
+            applied = spread(inc[2 * pair], inc[2 * pair + 1])
+            for h in range(2):
+                q = 2 * pair + h
+                work[q] = elem_scale * applied[h] + lam[q] * inc[q]
+        for side in range(2):
+            for pair in range(modes // 8):
+                applied = spread(far[side, 2 * pair], far[side, 2 * pair + 1])
+                for h in range(2):
+                    g = 2 * pair + h
+                    beside[side, g] = precv[side, 8] * applied[h] + precv[side, g] * far[side, g]
+        join_inner(work)
+        join_halo(work, beside, True, sweep < SWEEPS - 1)
+        for q in range(modes):
+            total = inc[q] + rate[q] * (res[q] - work[q])
+            if sweep < SWEEPS - 1:
+                inc[q] = total
+            else:
+                out[pl.ds(q, NODES, stride=modes), :] = fld[q] + total
         if sweep < SWEEPS - 1:
-            for q in range(modes):
-                fld[q] = fld[q] + rate[q] * res[q]
-            for pair in range(modes // 2):
-                for h, applied in enumerate(helmholtz(pair)):
-                    res[2 * pair + h] = load[2 * pair + h] - applied
-        else:
-            for q in range(modes):
-                out[pl.ds(q, NODES, stride=modes), :] = fld[q] + rate[q] * res[q]
+            for side in range(2):
+                for g in range(modes // 4):
+                    far[side, g] = far[side, g] + precv[side, 4 + g] * (
+                        halo[side, g] - beside[side, g]
+                    )
 
     for copies in (zcopy, xcopy):
         for copy in copies.values():
@@ -353,47 +451,13 @@
 ):
     modes = coeff.shape[1]
     planes = vel_axial.shape[1]
-    vmem = pl.BlockSpec(memory_space=pltpu.VMEM)
-    smem = pl.BlockSpec(memory_space=pltpu.SMEM)
-    anywhere = pl.BlockSpec(memory_space=pl.ANY)
     dma = pltpu.SemaphoreType.DMA
     field = pltpu.VMEM((modes, NODES, 128), F32)
     flat = pltpu.VMEM((NODES * modes, 128), F32)
-    result = pl.pallas_call(
-        functools.partial(kernel, modes),
-        out_shape=jax.ShapeDtypeStruct((NODES * modes, 128), F32),
-        in_specs=[
-            vmem, anywhere, anywhere, anywhere, anywhere, smem, smem, vmem, vmem, vmem, vmem, smem,
-            smem,
-        ],
-        out_specs=vmem,
-        scratch_shapes=[
-            pltpu.VMEM((3, 4, planes, 128), BF16),
-            pltpu.VMEM(tables.shape, BF16),
-            flat,
-            pltpu.VMEM((RING, 2, 3, 8 * modes, 128), F32),
-            pltpu.VMEM((RING * RING, 3, 4 * modes, 128), F32),
-            flat,
-            flat,
-            field,
-            field,
-            field,
-            field,
-            field,
-            pltpu.VMEM((SWEEPS + 1, 2, 2, SIDE, 128), F32),
-            pltpu.VMEM((SWEEPS + 1, 2, 2, SIDE, 128), F32),
-            dma((4,)),
-            dma((3, 2, 2)),
-            dma((3, 2, 2)),
-            dma((4, 3)),
-            dma((4, 3)),
-            dma((15,)),
-            dma((15,)),
-            dma((SWEEPS + 1, 2)),
-            dma((SWEEPS + 1, 2)),
-        ],
-        compiler_params=pltpu.CompilerParams(collective_id=0, has_side_effects=True),
-    )(
+    columns = pltpu.VMEM((2, modes // 4, NODES, 128), F32)
+    outer = pltpu.VMEM((2, modes // 2 + 1, NODES, 128), F32)
+    edges = pltpu.VMEM((2, 2, SIDE, 128), F32)
+    operands = (
         coeff.reshape(NODES * modes, 128),
         swirl_rate,
         vel_radial,
@@ -408,6 +472,54 @@
         wall_flag,
         transfer,
     )
+    result = pl.pallas_call(
+        functools.partial(kernel, modes),
+        out_shape=jax.ShapeDtypeStruct((NODES * modes, 128), F32),
+        in_specs=[pl.BlockSpec(memory_space=pl.ANY)] * len(operands),
+        out_specs=pl.BlockSpec(memory_space=pltpu.VMEM),
+        scratch_shapes=[
+            flat,
+            pltpu.SMEM(col_width.shape, F32),
+            pltpu.SMEM(row_height.shape, F32),
+            pltpu.VMEM((NODES, NODES), F32),
+            pltpu.VMEM((1, 128), F32),
+            pltpu.VMEM((NODES, 128), F32),
+            pltpu.VMEM((NODES, 128), F32),
+            pltpu.SMEM(wall_flag.shape, jnp.int32),
+            pltpu.SMEM(transfer.shape, F32),
+            pltpu.VMEM((3, 4, planes, 128), BF16),
+            pltpu.VMEM(tables.shape, BF16),
+            flat,
+            pltpu.VMEM((RING, 2, 3, 8 * modes, 128), F32),
+            pltpu.VMEM((RING * RING, 3, 4 * modes, 128), F32),
+            flat,
+            flat,
+            field,
+            field,
+            field,
+            field,
+            field,
+            field,
+            edges,
+            edges,
+            outer,
+            outer,
+            columns,
+            columns,
+            columns,
+            columns,
+            dma((13,)),
+            dma((3, 2, 2)),
+            dma((3, 2, 2)),
+            dma((4, 3)),
+            dma((4, 3)),
+            dma((15,)),
+            dma((15,)),
+            dma((3, 2)),
+            dma((3, 2)),
+        ],
+        compiler_params=pltpu.CompilerParams(collective_id=0, has_side_effects=True),
+    )(*operands)
     return result.reshape(coeff.shape)
 
 

time: 72.8 us -> 67 us (0.920)
  the two profiles are of different devices: /device:TPU:1 before, /device:TPU:57 now
where the time goes in v1:
time: 67 us; the launch traced here: 66.9 us
  Pallas kernels  65 us (97%)
  local copies, waits for them, and re-layouts  1.87 us (3%)
    pallas_call x1, Pallas kernels, local(): pl.pallas_call(functools.partial(kernel, modes), out_shape=jax.ShapeDtype...  65 us
    unnamed x1, local copies, waits for them, and re-layouts  1.87 us

profile of v1, /device:TPU:57, one launch (start us, length us, event | category | flops | bytes accessed | tf_op | source)
XLA Modules:
  0.0 66.9 jit_solution(13805384136867686419)
XLA Ops:
  0.0 65.0 %shard_map.127 = f32[1024,128]{1,0:T(8,128)} custom-call(f32[1024,128]{1,0:T(8,128)} %bitcast.4, bf16[4,256,128]{2,1,0:T(8,128)(2,1)} %vel_t.1, bf16[4,256,128]{2,1,0:T(8,128)(2,1)} %vel_y.1, bf16[4,256,128]{2,1,0:T(8,128)(2,1)} %vel_x.1, bf16[6,256,256]{2,1,0:T(8,128)(2,1)} %constant.2.clone.tables, f32[8]{0:T(128)} %width_in.1, f32[16]{0:T(128)} %height_in.1, ...), custom_call_target="tpu_custom_call" | custom-call | tf_op jit(solution)/shard_map/pallas_call | solution.py:475
  65.0 1.9 %copy.15 = f32[64,16,128]{2,1,0:T(8,128)} copy(f32[64,16,128]{2,1,0:T(8,128)} %bitcast.3) | data formatting | bytes 1048576

commit v2 on v1

v2 whole, which is shorter than its diff:
```python
import functools

import jax
import jax.numpy as jnp
import ml_dtypes
import numpy as np
from jax import lax
from jax.experimental import pallas as pl
from jax.experimental.pallas import tpu as pltpu
from jax.sharding import PartitionSpec as P

MESH = pl.DeviceIdType.MESH
SIDE = 8
NODES = 64
SWEEPS = 3
INV_STEP = 2.0
RELAX = 0.8
RING = 4
F32 = jnp.float32
BF16 = jnp.bfloat16


def cheb_matrix(side_count):
    points = np.cos(np.pi * np.arange(side_count) / (side_count - 1))
    weights = np.ones(side_count)
    weights[0] = weights[-1] = 2.0
    weights = weights * (-1.0) ** np.arange(side_count)
    table = np.zeros((side_count, side_count))
    for row in range(side_count):
        for col in range(side_count):
            if row != col:
                table[row, col] = weights[row] / weights[col] / (points[row] - points[col])
        table[row, row] = -np.sum(table[row])
    return table


def split_table(table):
    high = table.astype(np.float32).astype(ml_dtypes.bfloat16)
    low = (table - high.astype(np.float64)).astype(np.float32).astype(ml_dtypes.bfloat16)
    return [high, low]


def fourier_tables(planes):
    q = np.arange(planes)
    k = (q + 1) // 2
    angle = 2.0 * np.pi / planes * ((k[:, None] * np.arange(planes)[None, :]) % planes)
    sine = ((q % 2 == 0) & (q > 0))[:, None]
    wave = k[:, None].astype(np.float64)
    basis = np.where(sine, np.sin(angle), np.cos(angle))
    slope = np.where(sine, wave * np.cos(angle), -wave * np.sin(angle))
    norm = np.where((q == 0) | (q == planes - 1), 1.0, 2.0) / planes
    forward = basis * norm[:, None]
    return np.stack(split_table(slope.T) + split_table(basis.T) + split_table(forward))


def split(value):
    high = value.astype(BF16)
    return high, (value - high.astype(F32)).astype(BF16)


def dot3(tab_high, tab_low, value):
    high, low = split(value)
    total = jnp.dot(tab_high, high, preferred_element_type=F32)
    total += jnp.dot(tab_high, low, preferred_element_type=F32)
    return total + jnp.dot(tab_low, high, preferred_element_type=F32)


def kernel(
    modes, coeff_in, vel_t, vel_y, vel_x, tables, width_in, height_in, stiff_in, elem_in, mass_in,
    azim_in, flag_in, transfer_in, out,
    coeff, col_width, row_height, stiff, stiff_elem, traits, wall_flag, transfer,
    vel, tab, grad_y, zc, zg, zx, xc, xx, xy, hat, adv, fld, lam, rate, res, inc, work,
    theirs, side_lam, side_rate, tsend, halo, far, beside, local_sem, zs, zr, xs, xr, bs, br, hs, hr,
):
    s, m = lax.axis_index("elem"), lax.axis_index("mode")
    elems = lax.axis_size("elem")
    z, x = m // RING, m % RING
    cheb = cheb_matrix(SIDE)

    left, right = lax.max(s - 1, 0), lax.min(s + 1, elems - 1)
    has_left, has_right = s > 0, s < elems - 1
    barrier = pltpu.get_barrier_semaphore()
    for step in range(1, RING):
        pl.semaphore_signal(
            barrier, inc=1, device_id={"mode": (z + step) % RING * RING + x}, device_id_type=MESH
        )
        pl.semaphore_signal(
            barrier, inc=1, device_id={"mode": z * RING + (x + step) % RING}, device_id_type=MESH
        )
    for other, there in ((left, has_left), (right, has_right)):

        @pl.when(there)
        def _():
            pl.semaphore_signal(barrier, inc=1, device_id={"elem": other}, device_id_type=MESH)


    def fetch(pairs):
        copies = [
            pltpu.make_async_copy(src, dst, local_sem.at[i]) for i, (src, dst) in pairs
        ]
        for copy in copies:
            copy.start()
        return copies

    early = fetch(
        enumerate([(coeff_in, coeff), (height_in, row_height), (width_in, col_width)])
    )
    later = fetch(
        enumerate(
            [
                (stiff_in, stiff),
                (elem_in, stiff_elem),
                (mass_in, traits.at[pl.ds(0, NODES)]),
                (azim_in, traits.at[pl.ds(NODES, NODES)]),
                (flag_in, wall_flag),
                (transfer_in, transfer),
                (vel_t, vel.at[0]),
                (vel_y, vel.at[1]),
                (vel_x, vel.at[2]),
                (tables, tab),
            ],
            3,
        )
    )
    for copy in early:
        copy.wait()

    lane = lax.broadcasted_iota(jnp.int32, (1, 128), 1)
    col, row = lane // 16, lane % 16
    width = jnp.zeros((1, 128), F32)
    for a in range(8):
        width = jnp.where(col == a, col_width[a], width)
    height = jnp.zeros((1, 128), F32)
    for b in range(16):
        height = jnp.where(row == b, row_height[b], height)
    scale_x = 2.0 / width
    scale_y = 2.0 / height

    @pl.loop(0, SIDE)
    def _(i):
        start = pl.multiple_of(i * 16, 16)
        cells = [coeff[pl.ds(start + j * 128, 16), :] for j in range(SIDE)]
        place = pl.multiple_of(i % 4 // 2 * 64 + i // 4 * 32 + i % 2 * 16, 16)
        for j in range(SIDE):
            total = cheb[j, 0] * cells[0]
            for k in range(1, SIDE):
                total += cheb[j, k] * cells[k]
            grad_y[pl.ds(place + j * 128, 16), :] = total * scale_y

    pl.semaphore_wait(
        barrier, 2 * (RING - 1) + has_left.astype(jnp.int32) + has_right.astype(jnp.int32)
    )

    own_row = x // 2
    rows = (1 - own_row, own_row)
    zcopy, xcopy = {}, {}
    waves = [(rr, d) for rr in range(2) for d in (1, 3)] + [(rr, 2) for rr in range(2)]
    lots = ((1, 1), (2, 3), (3, 2))

    def row_start(plane, rr):
        return (plane * 2 + rows[rr]) * 128

    def start_z(what, d, rr, src, dst):
        copy = pltpu.make_async_remote_copy(
            src_ref=src,
            dst_ref=dst,
            send_sem=zs.at[what, d - 1, rr],
            recv_sem=zr.at[what, d - 1, rr],
            device_id={"mode": (z + d) % RING * RING + x},
            device_id_type=MESH,
        )
        copy.start()
        zcopy[what, d, rr] = copy

    def swap(pairs, turn_id):
        copies = []
        for side, other, there in ((0, left, has_left), (1, right, has_right)):
            copy = pltpu.make_async_remote_copy(
                src_ref=pairs[side][0],
                dst_ref=pairs[side][1],
                send_sem=hs.at[turn_id, side],
                recv_sem=hr.at[turn_id, 1 - side],
                device_id={"elem": other},
                device_id_type=MESH,
            )
            pl.when(there)(copy.start)
            copies.append(copy)
        return copies

    def settle(copies, theirs):
        for side, there in ((0, has_left), (1, has_right)):

            @pl.when(there)
            def _():
                copies[side].wait_send()
                copies[1 - side].wait_recv()

            @pl.when(jnp.logical_not(there))
            def _():
                theirs[side] = jnp.zeros(theirs.shape[1:], F32)

    for copy in later[:6]:
        copy.wait()
    flow = jnp.zeros((1, 128), F32)
    for a in range(8):
        flow = jnp.where(col == a, wall_flag[a].astype(F32) * transfer[a], flow)
    flow = jnp.where(row == 0, flow, 0.0)
    elem_scale = stiff_elem[...]
    line8 = lax.broadcasted_iota(jnp.int32, (SIDE, 128), 0)
    traits[2 * NODES : 2 * NODES + SIDE, :] = jnp.where(line8 == 0, elem_scale, flow)
    trait_copies = swap([(traits, theirs.at[1]), (traits, theirs.at[0])], 0)

    for rr, d in waves:
        at = pl.ds(pl.multiple_of(row_start((z + d) % RING, rr), 128), 128)
        start_z(0, d, rr, coeff.at[at], zc.at[z, rows[rr]])
    for part in range(2):
        for rr, d in waves:
            at = pl.ds(pl.multiple_of(row_start((z + d) % RING, rr) + 64 * part, 64), 64)
            start_z(1 + part, d, rr, grad_y.at[at], zg.at[z, rows[rr], part])

    partner = {1: x + 1 - 2 * (x % 2), 2: (x + 2) % RING, 3: RING - 1 - x}

    def start_x(what, k, mask, src, dst):
        copy = pltpu.make_async_remote_copy(
            src_ref=src,
            dst_ref=dst,
            send_sem=xs.at[what, k, mask - 1],
            recv_sem=xr.at[what, k, mask - 1],
            device_id={"mode": z * RING + partner[mask]},
            device_id_type=MESH,
        )
        copy.start()
        xcopy[what, k, mask] = copy

    def half(target, size):
        return pl.ds(pl.multiple_of(target % 2 * size, size), size)

    def pass_values(k, source, rr, line):
        cells = [line[16 * i : 16 * i + 16, :] for i in range(SIDE)]
        slopes = zx.at[source, rows[rr]]
        for i in range(SIDE):
            total = cheb[i, 0] * cells[0]
            for j in range(1, SIDE):
                total += cheb[i, j] * cells[j]
            slopes[16 * i : 16 * i + 16, :] = total * scale_x
        spot = source * RING + x
        for what, src, dst in ((0, line, xc), (1, slopes, xx)):
            for mask in (2, 3) if rr == 0 else (1,):
                start_x(what, k, mask, src.at[half(partner[mask], 64)], dst.at[spot])
            if rr == 1:
                dst[spot] = src[half(x, 64), :]

    def pass_grad(k, source, rr, part, line):
        spot = source * RING + x
        for mask in (2, 3) if rr == 0 else (1,):
            start_x(2 + part, k, mask, line.at[half(partner[mask], 32)], xy.at[spot, part])
        if rr == 1:
            xy[spot, part] = line[half(x, 32), :]

    for rr in range(2):
        at = pl.multiple_of(row_start(z, rr), 128)
        pass_values(0, z, rr, coeff.at[pl.ds(at, 128)])
        for part in range(2):
            pass_grad(0, z, rr, part, grad_y.at[pl.ds(at + 64 * part, 64)])

    ones = traits[0:NODES, :]
    weights = traits[NODES : 2 * NODES, :]
    node = lax.broadcasted_iota(jnp.int32, (NODES, 128), 0)
    stiffness = stiff[...]
    on_diag = lax.broadcasted_iota(jnp.int32, (NODES, NODES), 0) == lax.broadcasted_iota(
        jnp.int32, (NODES, NODES), 1
    )
    stiff_diag = jnp.sum(jnp.where(on_diag, stiffness, 0.0), axis=1, keepdims=True)
    stiff_high, stiff_low = split(stiffness)

    def spread(first, second):
        both = dot3(stiff_high, stiff_low, jnp.concatenate([first, second], axis=1))
        return both[:, :128], both[:, 128:]

    def local_terms(lumped, inverse, rates, scale, lam_to, diag_to):
        wall = jnp.where(node < SIDE, jnp.broadcast_to(rates, (NODES, 128)), 0.0)
        stiff_part = stiff_diag * scale
        for q in range(modes):
            wave = ((m * modes + q + 1) // 2).astype(F32) * (2.0 / (modes * RING * RING))
            value = (INV_STEP + (wave * wave) * inverse) * lumped + wall
            lam_to[q] = value
            diag_to[q] = stiff_part + value

    local_terms(ones, weights, flow, elem_scale, lam, rate)
    for q in range(modes):
        fld[q] = coeff[pl.ds(q, NODES, stride=modes), :]

    first_nodes = pl.ds(0, SIDE, stride=SIDE)
    last_nodes = pl.ds(SIDE - 1, SIDE, stride=SIDE)
    def turn(value, shift):
        return pltpu.roll(value, shift % 128, 1) if shift % 128 else value

    def join_rows(values, q):
        lower = values[q, 0:SIDE, :]
        upper = values[q, NODES - SIDE : NODES, :]
        values[q, 0:SIDE, :] = lower + jnp.where(row > 0, turn(upper, 1), 0.0)
        values[q, NODES - SIDE : NODES, :] = upper + jnp.where(row < 15, turn(lower, -1), 0.0)

    for pair in range(modes // 2):
        applied = spread(fld[2 * pair], fld[2 * pair + 1])
        for h in range(2):
            q = 2 * pair + h
            res[q] = (INV_STEP * ones - lam[q]) * fld[q] - elem_scale * applied[h]
    quad = lane // 32
    outer = col % 2

    def pack(pieces, send, shift):
        for g in range(len(pieces) // 4):
            total = None
            for k in range(4):
                piece = turn(pieces[4 * g + k], 32 * k + shift)
                total = piece if total is None else jnp.where(quad == k, piece, total)
            send[g] = total

    def join_inner(values):
        for q in range(modes):
            low, high = values[q, first_nodes, :], values[q, last_nodes, :]
            values[q, first_nodes, :] = low + jnp.where(col == 0, 0.0, turn(high, 16))
            values[q, last_nodes, :] = high + jnp.where(col == 7, 0.0, turn(low, -16))

    def join_halo(values, beside, inner, both):
        for g in range(modes // 4):
            left_low, left_high = beside[0, g, first_nodes, :], beside[0, g, last_nodes, :]
            right_low, right_high = beside[1, g, first_nodes, :], beside[1, g, last_nodes, :]
            add_left = turn(left_low, -16)
            add_right = turn(right_high, 16)
            for k in range(4):
                q = 4 * g + k
                low, high = values[q, first_nodes, :], values[q, last_nodes, :]
                near = turn(left_high, -32 * k - 16)
                past = turn(right_low, 112 - 32 * k)
                values[q, first_nodes, :] = jnp.where(col == 0, low + near, low)
                values[q, last_nodes, :] = jnp.where(col == 7, high + past, high)
                if both:
                    add_left = jnp.where(col == 2 * k + 1, turn(low, 32 * k + 16), add_left)
                    add_right = jnp.where(col == 2 * k, turn(high, 32 * k + 16), add_right)
            if both:
                if not inner:
                    add_left = jnp.where(outer == 1, add_left, 0.0)
                    add_right = jnp.where(outer == 0, add_right, 0.0)
                beside[0, g, last_nodes, :] = left_high + add_left
                beside[1, g, first_nodes, :] = right_low + add_right
                if inner:
                    beside[0, g, first_nodes, :] = left_low + jnp.where(
                        outer == 1, turn(left_high, 16), 0.0
                    )
                    beside[1, g, last_nodes, :] = right_high + jnp.where(
                        outer == 0, turn(right_low, -16), 0.0
                    )
        for q in range(modes):
            join_rows(values, q)
        if both:
            for side in range(2):
                for g in range(modes // 4):
                    join_rows(beside.at[side], g)

    for k, d in lots:
        source = (z - d + RING) % RING
        for rr in range(2):
            zcopy[0, d, rr].wait_recv()
            pass_values(k, source, rr, zc.at[source, rows[rr]])

    settle(trait_copies, theirs)
    join_inner(rate)
    side_scale = []
    here = lane >= 64
    for side in range(2):
        def window(mine, others):
            return jnp.where(here == (side == 0), turn(mine, 64), turn(others, 64))

        local_terms(
            window(ones, theirs[side, 0:NODES, :]),
            window(weights, theirs[side, NODES : 2 * NODES, :]),
            window(flow, theirs[side, 2 * NODES + 1 : 2 * NODES + 2, :]),
            window(elem_scale, theirs[side, 2 * NODES : 2 * NODES + 1, :]),
            work,
            inc,
        )
        join_inner(inc)
        for q in range(modes):
            at = first_nodes if side == 0 else last_nodes
            value = turn(inc[q, at, :], 64)
            rate[q, at, :] = jnp.where(col == (0 if side == 0 else 7), value, rate[q, at, :])
            join_rows(inc, q)
            inc[q] = RELAX / inc[q]
        shift = -32 if side == 0 else -64
        pack([work[q] for q in range(modes)], side_lam.at[side], shift)
        pack([inc[q] for q in range(modes)], side_rate.at[side], shift)

        @pl.when(jnp.logical_not(has_left if side == 0 else has_right))
        def _():
            side_rate[side] = jnp.zeros(side_rate.shape[1:], F32)

        scales = window(elem_scale, theirs[side, 2 * NODES : 2 * NODES + 1, :])
        total = None
        for k in range(4):
            piece = turn(scales, 32 * k + shift)
            total = piece if total is None else jnp.where(quad == k, piece, total)
        side_scale.append(total)
    for q in range(modes):
        join_rows(rate, q)
        rate[q] = RELAX / rate[q]

    bcopy = []
    for part in range(2):
        for k, d in lots:
            source = (z - d + RING) % RING
            for rr in range(2):
                zcopy[1 + part, d, rr].wait_recv()
                pass_grad(k, source, rr, part, zg.at[source, rows[rr], part])
        if part == 0:
            for copy in later[6:]:
                copy.wait()
        for (what, k, mask), copy in xcopy.items():
            if what == 2 + part or (what < 2 and part == 0):
                copy.wait_recv()
        advect = None
        for kind, src in enumerate((xc, xy, xx)):
            pieces = []
            for h in range(2):
                at = 32 * part + 16 * h
                piece = src[:, part, 16 * h : 16 * h + 16, :] if kind == 1 else src[:, at : at + 16, :]
                pieces.append(piece.reshape(-1, 128))
            which = 0 if kind == 0 else 2
            phys = dot3(tab[which], tab[which + 1], jnp.concatenate(pieces, axis=1))
            speed = jnp.concatenate([vel[kind, 2 * part], vel[kind, 2 * part + 1]], axis=1)
            term = speed.astype(F32) * phys
            advect = term if advect is None else advect + term
        back = dot3(tab[4], tab[5], advect)
        for h in range(2):
            for t in range(RING * RING):
                hat[part, t, 16 * h : 16 * h + 16, :] = back[
                    16 * t : 16 * t + 16, 128 * h : 128 * h + 128
                ]
        mine = pl.ds(pl.multiple_of(m * 64 + 32 * part, 32), 32)
        for d in range(1, RING * RING):
            target = (m + d) % (RING * RING)
            copy = pltpu.make_async_remote_copy(
                src_ref=hat.at[part, target],
                dst_ref=adv.at[mine],
                send_sem=bs.at[part, d - 1],
                recv_sem=br.at[part, d - 1],
                device_id={"mode": target},
                device_id_type=MESH,
            )
            copy.start()
            bcopy.append(copy)
        adv[mine, :] = hat[part, m]
    for copy in bcopy:
        copy.wait_recv()

    for q in range(modes):
        res[q] = res[q] - ones * adv[pl.ds(q, NODES, stride=modes), :]
    join_inner(res)
    for side in range(2):
        pack([res[q] for q in range(modes)], tsend.at[side], 32 * side)
    settle(swap([(tsend.at[0], halo.at[1]), (tsend.at[1], halo.at[0])], 1), halo)
    join_halo(res, halo, False, True)

    for q in range(modes):
        inc[q] = rate[q] * res[q]
    for side in range(2):
        for g in range(modes // 4):
            far[side, g] = side_rate[side, g] * halo[side, g]
    for sweep in range(1, SWEEPS):
        for pair in range(modes // 2):
            applied = spread(inc[2 * pair], inc[2 * pair + 1])
            for h in range(2):
                q = 2 * pair + h
                work[q] = elem_scale * applied[h] + lam[q] * inc[q]
        for side in range(2):
            for pair in range(modes // 8):
                applied = spread(far[side, 2 * pair], far[side, 2 * pair + 1])
                for h in range(2):
                    g = 2 * pair + h
                    beside[side, g] = side_scale[side] * applied[h] + side_lam[side, g] * far[side, g]
        join_inner(work)
        join_halo(work, beside, True, sweep < SWEEPS - 1)
        for q in range(modes):
            total = inc[q] + rate[q] * (res[q] - work[q])
            if sweep < SWEEPS - 1:
                inc[q] = total
            else:
                out[pl.ds(q, NODES, stride=modes), :] = fld[q] + total
        if sweep < SWEEPS - 1:
            for side in range(2):
                for g in range(modes // 4):
                    far[side, g] = far[side, g] + side_rate[side, g] * (
                        halo[side, g] - beside[side, g]
                    )

    for copies in (zcopy, xcopy):
        for copy in copies.values():
            copy.wait_send()
    for copy in bcopy:
        copy.wait_send()


def local(
    tables, coeff, vel_axial, vel_radial, swirl_rate, col_width, row_height, stiffness, stiff_elem,
    mass, azim_weight, wall_flag, transfer,
):
    modes = coeff.shape[1]
    planes = vel_axial.shape[1]
    dma = pltpu.SemaphoreType.DMA
    field = pltpu.VMEM((modes, NODES, 128), F32)
    flat = pltpu.VMEM((NODES * modes, 128), F32)
    columns = pltpu.VMEM((2, modes // 4, NODES, 128), F32)
    rows = pltpu.VMEM((RING, 2, 8 * modes, 128), F32)
    blocks = pltpu.VMEM((RING * RING, 4 * modes, 128), F32)
    halves = pltpu.VMEM((RING * RING, 2, 2 * modes, 128), F32)
    operands = (
        coeff.reshape(NODES * modes, 128),
        swirl_rate,
        vel_radial,
        vel_axial,
        jnp.asarray(tables),
        col_width,
        row_height,
        stiffness,
        stiff_elem.reshape(1, 128),
        mass,
        azim_weight,
        wall_flag,
        transfer,
    )
    result = pl.pallas_call(
        functools.partial(kernel, modes),
        out_shape=jax.ShapeDtypeStruct((NODES * modes, 128), F32),
        in_specs=[pl.BlockSpec(memory_space=pl.ANY)] * len(operands),
        out_specs=pl.BlockSpec(memory_space=pltpu.VMEM),
        scratch_shapes=[
            flat,
            pltpu.SMEM(col_width.shape, F32),
            pltpu.SMEM(row_height.shape, F32),
            pltpu.VMEM((NODES, NODES), F32),
            pltpu.VMEM((1, 128), F32),
            pltpu.VMEM((2 * NODES + SIDE, 128), F32),
            pltpu.SMEM(wall_flag.shape, jnp.int32),
            pltpu.SMEM(transfer.shape, F32),
            pltpu.VMEM((3, 4, planes, 128), BF16),
            pltpu.VMEM(tables.shape, BF16),
            flat,
            rows,
            pltpu.VMEM((RING, 2, 2, 4 * modes, 128), F32),
            rows,
            blocks,
            blocks,
            halves,
            pltpu.VMEM((2, RING * RING, 2 * modes, 128), F32),
            flat,
            field,
            field,
            field,
            field,
            field,
            field,
            pltpu.VMEM((2, 2 * NODES + SIDE, 128), F32),
            columns,
            columns,
            columns,
            columns,
            columns,
            columns,
            dma((13,)),
            dma((3, 3, 2)),
            dma((3, 3, 2)),
            dma((4, 4, 3)),
            dma((4, 4, 3)),
            dma((2, 15)),
            dma((2, 15)),
            dma((2, 2)),
            dma((2, 2)),
        ],
        compiler_params=pltpu.CompilerParams(collective_id=0, has_side_effects=True),
    )(*operands)
    return result.reshape(coeff.shape)


def solution(mesh):
    tables = fourier_tables(256)
    return jax.shard_map(
        functools.partial(local, tables),
        mesh=mesh,
        in_specs=(
            P(None, "mode", "elem"),
            P("mode", None, "elem"),
            P("mode", None, "elem"),
            P("mode", None, "elem"),
            P("elem"),
            P(),
            P(),
            P("elem"),
            P(None, "elem"),
            P(None, "elem"),
            P("elem"),
            P("elem"),
        ),
        out_specs=P(None, "mode", "elem"),
        check_vma=False,
    )
```

time: 67 us -> 62.6 us (0.934)
  the two profiles are of different devices: /device:TPU:57 before, /device:TPU:17 now
where the time goes in v2:
time: 62.6 us; the launch traced here: 62.2 us
  Pallas kernels  60.3 us (96%)
  local copies, waits for them, and re-layouts  1.87 us (3%)
    pallas_call x1, Pallas kernels, local(): pl.pallas_call(functools.partial(kernel, modes), out_shape=jax.ShapeDtype...  60.3 us
    unnamed x1, local copies, waits for them, and re-layouts  1.87 us

profile of v2, /device:TPU:17, one launch (start us, length us, event | category | flops | bytes accessed | tf_op | source)
XLA Modules:
  0.0 62.2 jit_solution(16868805614858110082)
XLA Ops:
  0.0 60.3 %shard_map.127 = f32[1024,128]{1,0:T(8,128)} custom-call(f32[1024,128]{1,0:T(8,128)} %bitcast.4, bf16[4,256,128]{2,1,0:T(8,128)(2,1)} %vel_t.1, bf16[4,256,128]{2,1,0:T(8,128)(2,1)} %vel_y.1, bf16[4,256,128]{2,1,0:T(8,128)(2,1)} %vel_x.1, bf16[6,256,256]{2,1,0:T(8,128)(2,1)} %constant.2.clone.tables, f32[8]{0:T(128)} %width_in.1, f32[16]{0:T(128)} %height_in.1, ...), custom_call_target="tpu_custom_call" | custom-call | tf_op jit(solution)/shard_map/pallas_call | solution.py:532
  60.3 1.9 %copy.15 = f32[64,16,128]{2,1,0:T(8,128)} copy(f32[64,16,128]{2,1,0:T(8,128)} %bitcast.3) | data formatting | bytes 1048576

commit v3 on v2

--- a/solution.py
+++ b/solution.py
@@ -69,7 +69,7 @@
     modes, coeff_in, vel_t, vel_y, vel_x, tables, width_in, height_in, stiff_in, elem_in, mass_in,
     azim_in, flag_in, transfer_in, out,
     coeff, col_width, row_height, stiff, stiff_elem, traits, wall_flag, transfer,
-    vel, tab, grad_y, zc, zg, zx, xc, xx, xy, hat, adv, fld, lam, rate, res, inc, work,
+    vel, tab, grad_y, ends, far_ends, zc, zg, zx, xc, xx, xy, hat, adv, fld, lam, rate, res, inc, work,
     theirs, side_lam, side_rate, tsend, halo, far, beside, local_sem, zs, zr, xs, xr, bs, br, hs, hr,
 ):
     s, m = lax.axis_index("elem"), lax.axis_index("mode")
@@ -81,9 +81,13 @@
     has_left, has_right = s > 0, s < elems - 1
     barrier = pltpu.get_barrier_semaphore()
     for step in range(1, RING):
-        pl.semaphore_signal(
-            barrier, inc=1, device_id={"mode": (z + step) % RING * RING + x}, device_id_type=MESH
-        )
+        if step != 2:
+            pl.semaphore_signal(
+                barrier,
+                inc=1,
+                device_id={"mode": (z + step) % RING * RING + x},
+                device_id_type=MESH,
+            )
         pl.semaphore_signal(
             barrier, inc=1, device_id={"mode": z * RING + (x + step) % RING}, device_id_type=MESH
         )
@@ -147,14 +151,29 @@
                 total += cheb[j, k] * cells[k]
             grad_y[pl.ds(place + j * 128, 16), :] = total * scale_y
 
-    pl.semaphore_wait(
-        barrier, 2 * (RING - 1) + has_left.astype(jnp.int32) + has_right.astype(jnp.int32)
-    )
-
     own_row = x // 2
     rows = (1 - own_row, own_row)
+    for plane in range(RING):
+        tile = jnp.zeros((16, 128), F32)
+        for kind, src in ((0, coeff), (1, grad_y)):
+            for rr in range(2):
+                at = pl.multiple_of((2 * plane + rows[rr]) * 128 + 112, 16)
+                edge = pltpu.roll(src[pl.ds(at, 16), :], 32 * kind + 16 * rr + 16, 1)
+                tile = jnp.where(col == 2 * kind + rr, edge, tile)
+        ends[16 * plane : 16 * plane + 16, :] = tile
+
+    def last_node(first, tile, which):
+        return jnp.where(
+            lane < 112, pltpu.roll(first, 112, 1), pltpu.roll(tile, 112 - 16 * which, 1)
+        )
+
+    pl.semaphore_wait(
+        barrier, 2 * RING - 3 + has_left.astype(jnp.int32) + has_right.astype(jnp.int32)
+    )
+
     zcopy, xcopy = {}, {}
-    waves = [(rr, d) for rr in range(2) for d in (1, 3)] + [(rr, 2) for rr in range(2)]
+    near = [(rr, d) for rr in range(2) for d in (1, 3)]
+    waves = near + [(rr, 2) for rr in range(2)]
     lots = ((1, 1), (2, 3), (3, 2))
 
     def row_start(plane, rr):
@@ -210,13 +229,15 @@
     traits[2 * NODES : 2 * NODES + SIDE, :] = jnp.where(line8 == 0, elem_scale, flow)
     trait_copies = swap([(traits, theirs.at[1]), (traits, theirs.at[0])], 0)
 
-    for rr, d in waves:
-        at = pl.ds(pl.multiple_of(row_start((z + d) % RING, rr), 128), 128)
-        start_z(0, d, rr, coeff.at[at], zc.at[z, rows[rr]])
-    for part in range(2):
-        for rr, d in waves:
-            at = pl.ds(pl.multiple_of(row_start((z + d) % RING, rr) + 64 * part, 64), 64)
-            start_z(1 + part, d, rr, grad_y.at[at], zg.at[z, rows[rr], part])
+    def send_values(d, rr):
+        if rr == 0:
+            at = pl.ds(pl.multiple_of((z + d) % RING * 16, 16), 16)
+            start_z(3, d, 0, ends.at[at], far_ends.at[z])
+        at = pl.ds(pl.multiple_of(row_start((z + d) % RING, rr), 128), 112)
+        start_z(0, d, rr, coeff.at[at], zc.at[z, rows[rr], pl.ds(0, 112)])
+
+    for rr, d in near:
+        send_values(d, rr)
 
     partner = {1: x + 1 - 2 * (x % 2), 2: (x + 2) % RING, 3: RING - 1 - x}
 
@@ -263,6 +284,14 @@
         for part in range(2):
             pass_grad(0, z, rr, part, grad_y.at[pl.ds(at + 64 * part, 64)])
 
+    zcopy[0, 1, 0].wait_recv()
+    for rr in range(2):
+        send_values(2, rr)
+    for part, size in ((0, 64), (1, 48)):
+        for rr, d in waves:
+            at = pl.ds(pl.multiple_of(row_start((z + d) % RING, rr) + 64 * part, 64), size)
+            start_z(1 + part, d, rr, grad_y.at[at], zg.at[z, rows[rr], part, pl.ds(0, size)])
+
     ones = traits[0:NODES, :]
     weights = traits[NODES : 2 * NODES, :]
     node = lax.broadcasted_iota(jnp.int32, (NODES, 128), 0)
@@ -272,9 +301,12 @@
     )
     stiff_diag = jnp.sum(jnp.where(on_diag, stiffness, 0.0), axis=1, keepdims=True)
     stiff_high, stiff_low = split(stiffness)
+    stiff_all = jnp.concatenate([stiff_high, stiff_high, stiff_low], axis=1)
 
     def spread(first, second):
-        both = dot3(stiff_high, stiff_low, jnp.concatenate([first, second], axis=1))
+        high, low = split(jnp.concatenate([first, second], axis=1))
+        cells = jnp.concatenate([high, low, high], axis=0)
+        both = jnp.dot(stiff_all, cells, preferred_element_type=F32)
         return both[:, :128], both[:, 128:]
 
     def local_terms(lumped, inverse, rates, scale, lam_to, diag_to):
@@ -362,7 +394,12 @@
     for k, d in lots:
         source = (z - d + RING) % RING
         for rr in range(2):
-            zcopy[0, d, rr].wait_recv()
+            if rr == 0:
+                zcopy[3, d, 0].wait_recv()
+            if (d, rr) != (1, 0):
+                zcopy[0, d, rr].wait_recv()
+            line = zc.at[source, rows[rr]]
+            line[112:128, :] = last_node(line[0:16, :], far_ends[source], rr)
             pass_values(k, source, rr, zc.at[source, rows[rr]])
 
     settle(trait_copies, theirs)
@@ -412,6 +449,9 @@
             source = (z - d + RING) % RING
             for rr in range(2):
                 zcopy[1 + part, d, rr].wait_recv()
+                if part == 1:
+                    line = zg.at[source, rows[rr]]
+                    line[1, 48:64, :] = last_node(line[0, 0:16, :], far_ends[source], 2 + rr)
                 pass_grad(k, source, rr, part, zg.at[source, rows[rr], part])
         if part == 0:
             for copy in later[6:]:
@@ -531,7 +571,7 @@
     )
     result = pl.pallas_call(
         functools.partial(kernel, modes),
-        out_shape=jax.ShapeDtypeStruct((NODES * modes, 128), F32),
+        out_shape=pltpu.VMEM((NODES * modes, 128), F32),
         in_specs=[pl.BlockSpec(memory_space=pl.ANY)] * len(operands),
         out_specs=pl.BlockSpec(memory_space=pltpu.VMEM),
         scratch_shapes=[
@@ -546,6 +586,8 @@
             pltpu.VMEM((3, 4, planes, 128), BF16),
             pltpu.VMEM(tables.shape, BF16),
             flat,
+            pltpu.VMEM((RING * modes, 128), F32),
+            pltpu.VMEM((RING, modes, 128), F32),
             rows,
             pltpu.VMEM((RING, 2, 2, 4 * modes, 128), F32),
             rows,
@@ -568,8 +610,8 @@
             columns,
             columns,
             dma((13,)),
-            dma((3, 3, 2)),
-            dma((3, 3, 2)),
+            dma((4, 3, 2)),
+            dma((4, 3, 2)),
             dma((4, 4, 3)),
             dma((4, 4, 3)),
             dma((2, 15)),

time: 62.6 us -> 59.3 us (0.947)
  Pallas kernels: 60.3 us -> 58.4 us
  local copies, waits for them, and re-layouts: 1.87 us -> 0.8 us
    pallas_call x1, Pallas kernels: 60.3 us -> 58.4 us  [local(): pl.pallas_call(functools.partial(kernel, modes), out_shape=pltpu.VMEM((NO...]
    unnamed x1, local copies, waits for them, and re-layouts: 1.87 us -> 0.8 us
where the time goes in v3:
time: 59.3 us; the launch traced here: 59.2 us
  Pallas kernels  58.4 us (98%)
  local copies, waits for them, and re-layouts  0.8 us (1%)
    pallas_call x1, Pallas kernels, local(): pl.pallas_call(functools.partial(kernel, modes), out_shape=pltpu.VMEM((NO...  58.4 us

profile of v3, /device:TPU:17, one launch (start us, length us, event | category | flops | bytes accessed | tf_op | source)
XLA Modules:
  0.0 59.2 jit_solution(981576650700791084)
XLA Ops:
  0.0 58.4 %shard_map.127 = f32[1024,128]{1,0:T(8,128)S(1)} custom-call(f32[1024,128]{1,0:T(8,128)} %bitcast.4, bf16[4,256,128]{2,1,0:T(8,128)(2,1)} %vel_t.1, bf16[4,256,128]{2,1,0:T(8,128)(2,1)} %vel_y.1, bf16[4,256,128]{2,1,0:T(8,128)(2,1)} %vel_x.1, bf16[6,256,256]{2,1,0:T(8,128)(2,1)} %constant.2.clone.tables, f32[8]{0:T(128)} %width_in.1, f32[16]{0:T(128)} %height_in.1, ...), custom_call_target="tpu_custom_call" | custom-call | tf_op jit(solution)/shard_map/pallas_call | solution.py:572
  58.4 0.8 %copy.15 = f32[64,16,128]{2,1,0:T(8,128)} copy(f32[64,16,128]{2,1,0:T(8,128)S(1)} %bitcast.3) | data formatting | bytes 1048576

commit v4 on v3

--- a/solution.py
+++ b/solution.py
@@ -69,7 +69,7 @@
     modes, coeff_in, vel_t, vel_y, vel_x, tables, width_in, height_in, stiff_in, elem_in, mass_in,
     azim_in, flag_in, transfer_in, out,
     coeff, col_width, row_height, stiff, stiff_elem, traits, wall_flag, transfer,
-    vel, tab, grad_y, ends, far_ends, zc, zg, zx, xc, xx, xy, hat, adv, fld, lam, rate, res, inc, work,
+    vel, tab, grad_y, ends, far_ends, zc, zg, zx, xc, xx, xy, partial, hat, adv, fld, lam, rate, res, inc, work,
     theirs, side_lam, side_rate, tsend, halo, far, beside, local_sem, zs, zr, xs, xr, bs, br, hs, hr,
 ):
     s, m = lax.axis_index("elem"), lax.axis_index("mode")
@@ -288,7 +288,7 @@
     for rr in range(2):
         send_values(2, rr)
     for part, size in ((0, 64), (1, 48)):
-        for rr, d in waves:
+        for rr, d in waves[4:] + waves[:4]:
             at = pl.ds(pl.multiple_of(row_start((z + d) % RING, rr) + 64 * part, 64), size)
             start_z(1 + part, d, rr, grad_y.at[at], zg.at[z, rows[rr], part, pl.ds(0, size)])
 
@@ -443,6 +443,8 @@
         join_rows(rate, q)
         rate[q] = RELAX / rate[q]
 
+    order = [(2, dx) for dx in (2, 1, 3, 0)]
+    order += [(dz, dx) for dx in (2, 1, 3, 0) for dz in (1, 3)] + [(0, dx) for dx in (2, 1, 3)]
     bcopy = []
     for part in range(2):
         for k, d in lots:
@@ -456,11 +458,12 @@
         if part == 0:
             for copy in later[6:]:
                 copy.wait()
-        for (what, k, mask), copy in xcopy.items():
-            if what == 2 + part or (what < 2 and part == 0):
-                copy.wait_recv()
-        advect = None
-        for kind, src in enumerate((xc, xy, xx)):
+        if part == 0:
+            for (what, k, mask), copy in xcopy.items():
+                if what < 2:
+                    copy.wait_recv()
+
+        def advection(kind, src):
             pieces = []
             for h in range(2):
                 at = 32 * part + 16 * h
@@ -469,8 +472,13 @@
             which = 0 if kind == 0 else 2
             phys = dot3(tab[which], tab[which + 1], jnp.concatenate(pieces, axis=1))
             speed = jnp.concatenate([vel[kind, 2 * part], vel[kind, 2 * part + 1]], axis=1)
-            term = speed.astype(F32) * phys
-            advect = term if advect is None else advect + term
+            return speed.astype(F32) * phys
+
+        partial[...] = advection(0, xc) + advection(2, xx)
+        for (what, k, mask), copy in xcopy.items():
+            if what == 2 + part:
+                copy.wait_recv()
+        advect = partial[...] + advection(1, xy)
         back = dot3(tab[4], tab[5], advect)
         for h in range(2):
             for t in range(RING * RING):
@@ -478,8 +486,8 @@
                     16 * t : 16 * t + 16, 128 * h : 128 * h + 128
                 ]
         mine = pl.ds(pl.multiple_of(m * 64 + 32 * part, 32), 32)
-        for d in range(1, RING * RING):
-            target = (m + d) % (RING * RING)
+        for d, (dz, dx) in enumerate(order, 1):
+            target = (z + dz) % RING * RING + (x + dx) % RING
             copy = pltpu.make_async_remote_copy(
                 src_ref=hat.at[part, target],
                 dst_ref=adv.at[mine],
@@ -594,6 +602,7 @@
             blocks,
             blocks,
             halves,
+            pltpu.VMEM((planes, 256), F32),
             pltpu.VMEM((2, RING * RING, 2 * modes, 128), F32),
             flat,
             field,

time: 59.3 us -> 57.5 us (0.970)
  Pallas kernels: 58.4 us -> 56.6 us
    pallas_call x1, Pallas kernels: 58.4 us -> 56.6 us  [local(): pl.pallas_call(functools.partial(kernel, modes), out_shape=pltpu.VMEM((NO...]
where the time goes in v4:
time: 57.5 us; the launch traced here: 57.4 us
  Pallas kernels  56.6 us (98%)
  local copies, waits for them, and re-layouts  0.8 us (1%)
    pallas_call x1, Pallas kernels, local(): pl.pallas_call(functools.partial(kernel, modes), out_shape=pltpu.VMEM((NO...  56.6 us

profile of v4, /device:TPU:17, one launch (start us, length us, event | category | flops | bytes accessed | tf_op | source)
XLA Modules:
  0.0 57.4 jit_solution(525838071911102994)
XLA Ops:
  0.0 56.6 %shard_map.127 = f32[1024,128]{1,0:T(8,128)S(1)} custom-call(f32[1024,128]{1,0:T(8,128)} %bitcast.4, bf16[4,256,128]{2,1,0:T(8,128)(2,1)} %vel_t.1, bf16[4,256,128]{2,1,0:T(8,128)(2,1)} %vel_y.1, bf16[4,256,128]{2,1,0:T(8,128)(2,1)} %vel_x.1, bf16[6,256,256]{2,1,0:T(8,128)(2,1)} %constant.2.clone.tables, f32[8]{0:T(128)} %width_in.1, f32[16]{0:T(128)} %height_in.1, ...), custom_call_target="tpu_custom_call" | custom-call | tf_op jit(solution)/shard_map/pallas_call | solution.py:580
  56.6 0.8 %copy.15 = f32[64,16,128]{2,1,0:T(8,128)} copy(f32[64,16,128]{2,1,0:T(8,128)S(1)} %bitcast.3) | data formatting | bytes 1048576

commit v5 on v4

--- a/solution.py
+++ b/solution.py
@@ -70,7 +70,7 @@
     azim_in, flag_in, transfer_in, out,
     coeff, col_width, row_height, stiff, stiff_elem, traits, wall_flag, transfer,
     vel, tab, grad_y, ends, far_ends, zc, zg, zx, xc, xx, xy, partial, hat, adv, fld, lam, rate, res, inc, work,
-    theirs, side_lam, side_rate, tsend, halo, far, beside, local_sem, zs, zr, xs, xr, bs, br, hs, hr,
+    theirs, side_lam, side_rate, tsend, halo, far, beside, local_sem, zs, zr, xs, xr, gs, gr, bs, br, hs, hr,
 ):
     s, m = lax.axis_index("elem"), lax.axis_index("mode")
     elems = lax.axis_size("elem")
@@ -144,7 +144,8 @@
     def _(i):
         start = pl.multiple_of(i * 16, 16)
         cells = [coeff[pl.ds(start + j * 128, 16), :] for j in range(SIDE)]
-        place = pl.multiple_of(i % 4 // 2 * 64 + i // 4 * 32 + i % 2 * 16, 16)
+        later_pair = ((i // 2 + 1) // 2 + 1) % 2
+        place = pl.multiple_of(later_pair * 64 + i // 4 * 32 + i % 2 * 16, 16)
         for j in range(SIDE):
             total = cheb[j, 0] * cells[0]
             for k in range(1, SIDE):
@@ -239,6 +240,30 @@
     for rr, d in near:
         send_values(d, rr)
 
+    order = [(2, dx) for dx in (2, 1, 3, 0)]
+    order += [(dz, dx) for dx in (2, 1, 3, 0) for dz in (1, 3)] + [(0, dx) for dx in (2, 1, 3)]
+    gcopy = []
+
+    def first_pair(plane, place):
+        return pl.ds(
+            pl.multiple_of((plane * 2 + place // 2) * 128 + place % 2 * 32, 32), 32
+        )
+
+    def send_first_pairs():
+        for d, (dz, dx) in enumerate(order):
+            plane, place = (z + dz) % RING, (x + dx) % RING
+            copy = pltpu.make_async_remote_copy(
+                src_ref=grad_y.at[first_pair(plane, place)],
+                dst_ref=xy.at[m, 0],
+                send_sem=gs.at[d],
+                recv_sem=gr.at[d],
+                device_id={"mode": plane * RING + place},
+                device_id_type=MESH,
+            )
+            copy.start()
+            gcopy.append(copy)
+        xy[m, 0] = grad_y[first_pair(z, x), :]
+
     partner = {1: x + 1 - 2 * (x % 2), 2: (x + 2) % RING, 3: RING - 1 - x}
 
     def start_x(what, k, mask, src, dst):
@@ -271,27 +296,21 @@
             if rr == 1:
                 dst[spot] = src[half(x, 64), :]
 
-    def pass_grad(k, source, rr, part, line):
+    def pass_grad(k, source, rr, line):
         spot = source * RING + x
         for mask in (2, 3) if rr == 0 else (1,):
-            start_x(2 + part, k, mask, line.at[half(partner[mask], 32)], xy.at[spot, part])
+            start_x(2, k, mask, line.at[half(partner[mask], 32)], xy.at[spot, 1])
         if rr == 1:
-            xy[spot, part] = line[half(x, 32), :]
+            xy[spot, 1] = line[half(x, 32), :]
 
     for rr in range(2):
         at = pl.multiple_of(row_start(z, rr), 128)
         pass_values(0, z, rr, coeff.at[pl.ds(at, 128)])
-        for part in range(2):
-            pass_grad(0, z, rr, part, grad_y.at[pl.ds(at + 64 * part, 64)])
+        pass_grad(0, z, rr, grad_y.at[pl.ds(at + 64, 64)])
 
     zcopy[0, 1, 0].wait_recv()
     for rr in range(2):
         send_values(2, rr)
-    for part, size in ((0, 64), (1, 48)):
-        for rr, d in waves[4:] + waves[:4]:
-            at = pl.ds(pl.multiple_of(row_start((z + d) % RING, rr) + 64 * part, 64), size)
-            start_z(1 + part, d, rr, grad_y.at[at], zg.at[z, rows[rr], part, pl.ds(0, size)])
-
     ones = traits[0:NODES, :]
     weights = traits[NODES : 2 * NODES, :]
     node = lax.broadcasted_iota(jnp.int32, (NODES, 128), 0)
@@ -400,7 +419,15 @@
                 zcopy[0, d, rr].wait_recv()
             line = zc.at[source, rows[rr]]
             line[112:128, :] = last_node(line[0:16, :], far_ends[source], rr)
-            pass_values(k, source, rr, zc.at[source, rows[rr]])
+            pass_values(k, source, rr, line)
+        if k == 2:
+            for mask in (1, 2, 3):
+                xcopy[0, 0, mask].wait_recv()
+                xcopy[0, 1, mask].wait_recv()
+            send_first_pairs()
+            for rr, d in waves[4:] + waves[:4]:
+                at = pl.multiple_of(row_start((z + d) % RING, rr) + 64, 64)
+                start_z(2, d, rr, grad_y.at[pl.ds(at, 48)], zg.at[z, rows[rr], pl.ds(0, 48)])
 
     settle(trait_copies, theirs)
     join_inner(rate)
@@ -443,41 +470,45 @@
         join_rows(rate, q)
         rate[q] = RELAX / rate[q]
 
-    order = [(2, dx) for dx in (2, 1, 3, 0)]
-    order += [(dz, dx) for dx in (2, 1, 3, 0) for dz in (1, 3)] + [(0, dx) for dx in (2, 1, 3)]
     bcopy = []
     for part in range(2):
-        for k, d in lots:
+        which_pair = (part + 1 + x % 2) % 2
+        for k, d in lots if part == 1 else ():
             source = (z - d + RING) % RING
             for rr in range(2):
-                zcopy[1 + part, d, rr].wait_recv()
-                if part == 1:
-                    line = zg.at[source, rows[rr]]
-                    line[1, 48:64, :] = last_node(line[0, 0:16, :], far_ends[source], 2 + rr)
-                pass_grad(k, source, rr, part, zg.at[source, rows[rr], part])
+                zcopy[2, d, rr].wait_recv()
+                line = zg.at[source, rows[rr]]
+                line[48:64, :] = last_node(line[0:16, :], far_ends[source], 2 + rr)
+                pass_grad(k, source, rr, line)
         if part == 0:
             for copy in later[6:]:
                 copy.wait()
         if part == 0:
             for (what, k, mask), copy in xcopy.items():
-                if what < 2:
+                if what < 2 and (what, k) not in ((0, 0), (0, 1)):
                     copy.wait_recv()
 
         def advection(kind, src):
             pieces = []
             for h in range(2):
-                at = 32 * part + 16 * h
-                piece = src[:, part, 16 * h : 16 * h + 16, :] if kind == 1 else src[:, at : at + 16, :]
+                at = pl.ds(pl.multiple_of(32 * which_pair + 16 * h, 16), 16)
+                piece = src[:, part, 16 * h : 16 * h + 16, :] if kind == 1 else src[:, at, :]
                 pieces.append(piece.reshape(-1, 128))
             which = 0 if kind == 0 else 2
             phys = dot3(tab[which], tab[which + 1], jnp.concatenate(pieces, axis=1))
-            speed = jnp.concatenate([vel[kind, 2 * part], vel[kind, 2 * part + 1]], axis=1)
+            speed = jnp.concatenate(
+                [vel[kind, 2 * which_pair], vel[kind, 2 * which_pair + 1]], axis=1
+            )
             return speed.astype(F32) * phys
 
         partial[...] = advection(0, xc) + advection(2, xx)
-        for (what, k, mask), copy in xcopy.items():
-            if what == 2 + part:
+        if part == 0:
+            for copy in gcopy:
                 copy.wait_recv()
+        else:
+            for (what, k, mask), copy in xcopy.items():
+                if what == 2:
+                    copy.wait_recv()
         advect = partial[...] + advection(1, xy)
         back = dot3(tab[4], tab[5], advect)
         for h in range(2):
@@ -485,7 +516,7 @@
                 hat[part, t, 16 * h : 16 * h + 16, :] = back[
                     16 * t : 16 * t + 16, 128 * h : 128 * h + 128
                 ]
-        mine = pl.ds(pl.multiple_of(m * 64 + 32 * part, 32), 32)
+        mine = pl.ds(pl.multiple_of(m * 64 + 32 * which_pair, 32), 32)
         for d, (dz, dx) in enumerate(order, 1):
             target = (z + dz) % RING * RING + (x + dx) % RING
             copy = pltpu.make_async_remote_copy(
@@ -545,7 +576,7 @@
     for copies in (zcopy, xcopy):
         for copy in copies.values():
             copy.wait_send()
-    for copy in bcopy:
+    for copy in gcopy + bcopy:
         copy.wait_send()
 
 
@@ -597,7 +628,7 @@
             pltpu.VMEM((RING * modes, 128), F32),
             pltpu.VMEM((RING, modes, 128), F32),
             rows,
-            pltpu.VMEM((RING, 2, 2, 4 * modes, 128), F32),
+            pltpu.VMEM((RING, 2, 4 * modes, 128), F32),
             rows,
             blocks,
             blocks,
@@ -621,8 +652,10 @@
             dma((13,)),
             dma((4, 3, 2)),
             dma((4, 3, 2)),
-            dma((4, 4, 3)),
-            dma((4, 4, 3)),
+            dma((3, 4, 3)),
+            dma((3, 4, 3)),
+            dma((15,)),
+            dma((15,)),
             dma((2, 15)),
             dma((2, 15)),
             dma((2, 2)),

time: 57.5 us -> 56.2 us (0.977)
  Pallas kernels: 56.6 us -> 55 us
    pallas_call x1, Pallas kernels: 56.6 us -> 55 us  [local(): pl.pallas_call(functools.partial(kernel, modes), out_shape=pltpu.VMEM((NO...]
where the time goes in v5:
time: 56.2 us; the launch traced here: 55.8 us
  Pallas kernels  55 us (98%)
  local copies, waits for them, and re-layouts  0.8 us (1%)
    pallas_call x1, Pallas kernels, local(): pl.pallas_call(functools.partial(kernel, modes), out_shape=pltpu.VMEM((NO...  55 us

profile of v5, /device:TPU:17, one launch (start us, length us, event | category | flops | bytes accessed | tf_op | source)
XLA Modules:
  0.0 55.8 jit_solution(8198984437866972499)
XLA Ops:
  0.0 55.0 %shard_map.127 = f32[1024,128]{1,0:T(8,128)S(1)} custom-call(f32[1024,128]{1,0:T(8,128)} %bitcast.4, bf16[4,256,128]{2,1,0:T(8,128)(2,1)} %vel_t.1, bf16[4,256,128]{2,1,0:T(8,128)(2,1)} %vel_y.1, bf16[4,256,128]{2,1,0:T(8,128)(2,1)} %vel_x.1, bf16[6,256,256]{2,1,0:T(8,128)(2,1)} %constant.2.clone.tables, f32[8]{0:T(128)} %width_in.1, f32[16]{0:T(128)} %height_in.1, ...), custom_call_target="tpu_custom_call" | custom-call | tf_op jit(solution)/shard_map/pallas_call | solution.py:611
  55.0 0.8 %copy.15 = f32[64,16,128]{2,1,0:T(8,128)} copy(f32[64,16,128]{2,1,0:T(8,128)S(1)} %bitcast.3) | data formatting | bytes 1048576
